TPU v7x, 128 devices: a whole 4x4x4 slice. The times are simulated.
128 devices in a mesh: grp: 8 (over z, core), sub: 16 (over x, y).
Axes of the slice: x: 4, y: 4, z: 4, core: 2. Of those that a mesh axis runs over, the one named last changes fastest.
Arguments:
- rhs: float32 [96, 131072], P(None, ('grp', 'sub')), may hold values from -13 to 13
- blocks: bfloat16 [16384, 6656], P(('grp', 'sub')), may hold values from -0.05 to 0.45, as said below
- owners: int32 [16384, 1], P(('grp', 'sub')), may hold values from 0 to 7; in each aligned block of 128 rows (0 to 127, 128 to 255, ...) at most 48 rows name the same one
- conn: int32 [16384, 27], P(('grp', 'sub')), may hold values from 0 to 16383, as said below
Outputs:
- solution: float32 [96, 131072], P(None, ('grp', 'sub'))
- residual: float32 [96, 131072], P(None, ('grp', 'sub'))
Inputs may be any that keep to these rules, and one draw needn't show every extreme that they name: `blocks`: entries at positions 6561 and beyond are zero. `owners`: in each device's 128 rows at most 48 name the same column. `conn`: A column's nodes form layers of 128 nodes, node n in layer n // 128. An element in the rows of the device at position s along sub touches three consecutive layers, all within nodes s * 1024 to (s + 1) * 1024 + 2 * 128 - 1 of its column (within the column).
All inputs are finite; a program needn't handle non-finite values.
Results may differ from a plain program's by a relative error of at most 0.0075.
Values may be sent and summed in bfloat16 or wider, within the bound.
A program may use at most 192 MiB of HBM per device.

v0:
```python
import jax
import jax.numpy as jnp
from jax import lax
from jax.sharding import PartitionSpec as P

STEPS = 2
epsilon = 1e-06


def passed_along(block, axis, distance):
    devices = range(lax.axis_size(axis))
    route = [(i - distance, i) for i in devices if i - distance in devices]
    return lax.ppermute(block, axis, route)


def place_blocks(blocks, owners, conn, groups, capacity):
    owner_group = owners[:, 0]
    onehot = (owner_group[:, None] == jnp.arange(groups, dtype=jnp.int32)[None, :]).astype(
        jnp.int32
    )
    before = jnp.cumsum(onehot, axis=0) - onehot
    position = jnp.sum(before * onehot, axis=1)
    target = owner_group * capacity + position
    send_blocks = (
        jnp.zeros((groups * capacity, blocks.shape[1]), blocks.dtype).at[target].set(blocks)
    )
    send_links = jnp.zeros((groups * capacity, conn.shape[1]), jnp.int32).at[target].set(conn)
    return (send_blocks.reshape(groups, capacity, -1), send_links.reshape(groups, capacity, -1))


def window_product(matrix_groups, link_groups, field):
    rows = field.shape[0]
    window = field.shape[1]
    places = jnp.arange(window, dtype=jnp.int32)

    def one_group(acc, pair):
        matrix, links = pair
        slot_count = matrix.shape[0]
        selector = (links[:, None] == places[None, :]).astype(jnp.bfloat16)
        picked = jnp.einsum(
            "rw,lw->rl", field, selector, preferred_element_type=jnp.float32
        ).astype(jnp.bfloat16)
        picked = picked.reshape(3, rows // 3, slot_count, 27)
        result = jnp.einsum("spcqd,cosp->dosq", matrix, picked, preferred_element_type=jnp.float32)
        result = result.reshape(rows, slot_count * 27)
        high_part = result.astype(jnp.bfloat16)
        low_part = (result - high_part.astype(jnp.float32)).astype(jnp.bfloat16)
        acc = acc + jnp.dot(high_part, selector, preferred_element_type=jnp.float32)
        acc = acc + jnp.dot(low_part, selector, preferred_element_type=jnp.float32)
        return (acc, None)

    start = jnp.zeros((rows, window), jnp.float32)
    acc, unused = lax.scan(one_group, start, (matrix_groups, link_groups))
    return acc


def column_sums(first, second):
    return jnp.sum((first * second).reshape(3, -1, first.shape[1]), axis=(0, 2))


def update(solution, residual, image, along, energy):
    alpha = along / (energy + epsilon)
    scale_rows = jnp.tile(alpha, 3)[:, None]
    return (solution + scale_rows * residual, residual - scale_rows * image)


def shards(rhs, blocks, owners, conn):
    groups = lax.axis_size("grp")
    held = blocks.shape[0]
    capacity = max(2, 3 * held // 8)
    send_blocks, send_links = place_blocks(blocks, owners, conn, groups, capacity)
    got_blocks, got_links = (
        lax.all_to_all(send_blocks, "grp", split_axis=0, concat_axis=0, tiled=True),
        lax.all_to_all(send_links, "grp", split_axis=0, concat_axis=0, tiled=True),
    )
    matrix_groups = got_blocks[:, :, :6561].reshape(groups, capacity, 27, 3, 27, 3)
    residual = rhs
    solution = jnp.zeros(rhs.shape, jnp.float32)
    own_count = rhs.shape[1]
    band_width = 2 * held
    local_links = jnp.clip(
        got_links - lax.axis_index("sub") * own_count, 0, own_count + band_width - 1
    ).astype(jnp.int32)
    link_groups = local_links.reshape(groups, capacity * 27)
    for step in range(STEPS):
        rounded = residual.astype(jnp.bfloat16)
        upper = passed_along(rounded[:, :band_width], "sub", -1)
        field = jnp.concatenate([rounded, upper], axis=1)
        partial_sum = window_product(matrix_groups, link_groups, field)
        incoming = passed_along(partial_sum[:, own_count:], "sub", 1)
        image = partial_sum[:, :own_count] + jnp.pad(
            incoming, ((0, 0), (0, own_count - band_width))
        )
        along, energy = lax.psum(
            (column_sums(residual, image), column_sums(image, image)), ("grp", "sub")
        )
        solution, residual = update(solution, residual, image, along, energy)
    return (solution, residual)


def solution(mesh):
    return jax.shard_map(
        shards,
        mesh=mesh,
        in_specs=(
            P(None, ("grp", "sub")),
            P(("grp", "sub"), None),
            P(("grp", "sub"), None),
            P(("grp", "sub"), None),
        ),
        out_specs=(P(None, ("grp", "sub")), P(None, ("grp", "sub"))),
        check_vma=False,
    )
```

profile of v0, /device:TPU:1, one launch (start us, length us, event | category | flops | bytes accessed | tf_op | source)
XLA Modules:
  0.0 515.8 jit_solution(13757841406392980905)
XLA Ops:
  5.7 6.8 %all-to-all-start = ((s32[8,1,1296]{2,1,0:T(1,128)}), s32[8,1,1296]{2,1,0:T(1,128)S(1)}, u32[]{:S(2)}, u32[]{:S(2)}) async-start(s32[8,1,1296]{2,1,0:T(1,128)} %reshape.81), calls=%async_computation | async-start | bytes 90112 | tf_op jit(solution)/shard_map/all_to_all | solution.py:74
  12.5 6.9 %scatter_custom_fusion.1 = bf16[384,6656]{1,0:T(8,128)(2,1)} fusion(s32[128]{0:T(128)S(1)} %fusion.50, bf16[128,6656]{1,0:T(8,128)(2,1)} %param.9, bf16[]{:T(256)} %constant.23.clone.1), kind=kCustom, calls=%fused_computation.46 | custom fusion | bytes 5112320 | tf_op jit(solution)/shard_map/scatter | solution.py:25
  19.5 4.9 all-to-all-start.1
  29.8 53.3 %all-to-all-done.1 = bf16[8,48,6656]{2,1,0:T(8,128)(2,1)} async-done(((bf16[8,48,6656]{2,1,0:T(8,128)(2,1)}), bf16[8,48,6656]{2,1,0:T(8,128)(2,1)}, u32[]{:S(2)}, u32[]{:S(2)}) %all-to-all-start.1) | async-done | bytes 5111840 | tf_op jit(solution)/shard_map/all_to_all | solution.py:73
  83.1 14.8 %copy.45 = bf16[8,48,6561]{1,0,2:T(8,128)(2,1)} copy(bf16[8,48,6561]{2,1,0:T(8,128)(2,1)} %bitcast.44) | data formatting | bytes 10077696
  97.9 35.7 %copy.35 = bf16[8,48,27,3,27,3]{4,2,3,5,1,0:T(8,128)(2,1)} copy(bf16[8,48,27,3,27,3]{1,0,5,4,3,2:T(8,128)(2,1)} %bitcast.67) | data formatting | bytes 10077696
  133.6 112.3 %while.22 = (s32[]{:T(128)}, f32[96,1280]{1,0:T(8,128)}, s32[8,1296]{1,0:T(8,128)}, bf16[96,1280]{1,0:T(8,128)(2,1)S(1)}, bf16[8,48,27,3,27,3]{4,2,3,5,1,0:T(8,128)(2,1)}, /*index=5*/s32[]{:T(128)}, s32[]{:T(128)}) while((s32[]{:T(128)}, f32[96,1280]{1,0:T(8,128)}, s32[8,1296]{1,0:T(8,128)}, bf16[96,1280]{1,0:T(8,128)(2,1)S(1)}, ...), condition=%wide.region_5.6_spmd.clone, body=%wide.region_4.5_spmd.clone.sunk | while | flops 981762048 | bytes 10256283 | solution.py:53
  137.7 2.8 fusion.75
  150.8 2.8 fusion.75
  165.0 2.8 fusion.75
  179.1 2.8 fusion.75
  193.3 2.8 fusion.75
  207.5 2.8 fusion.75
  221.6 2.8 fusion.75
  235.8 2.8 fusion.75
  246.8 3.2 collective-permute-start.1
  253.0 66.9 %all-reduce.3 = (f32[32]{0:T(128)S(1)}, f32[32]{0:T(128)S(1)}) all-reduce(f32[32]{0:T(128)S(1)} %reduce_sum.62, f32[32]{0:T(128)S(1)} %reduce_sum.82), channel_id=1, replica_groups=mesh['grp'=8,'sub'=16] {'grp','sub'}, use_global_device_ids=true, to_apply=%region_8.9 | all-reduce | flops 64 | bytes 512 | tf_op jit(solution)/shard_map/psum | solution.py:94
  323.4 3.3 collective-permute-done.2
  326.7 112.3 %while.23 = (s32[]{:T(128)}, f32[96,1280]{1,0:T(8,128)}, s32[8,1296]{1,0:T(8,128)}, bf16[96,1280]{1,0:T(8,128)(2,1)S(1)}, bf16[8,48,27,3,27,3]{4,2,3,5,1,0:T(8,128)(2,1)}, /*index=5*/s32[]{:T(128)}, s32[]{:T(128)}) while((s32[]{:T(128)}, f32[96,1280]{1,0:T(8,128)}, s32[8,1296]{1,0:T(8,128)}, bf16[96,1280]{1,0:T(8,128)(2,1)S(1)}, ...), condition=%wide.region_13.14_spmd.clone, body=%wide.region_12.13_spmd.clone.sunk | while | flops 981762048 | bytes 10256283 | solution.py:53
  330.8 2.8 fusion.83
  343.9 2.8 fusion.83
  358.1 2.8 fusion.83
  372.3 2.8 fusion.83
  445.6 68.0 %all-reduce.2 = (f32[32]{0:T(128)S(1)}, f32[32]{0:T(128)S(1)}) all-reduce(f32[32]{0:T(128)S(1)} %reduce_sum.85, f32[32]{0:T(128)S(1)} %reduce_sum.88), channel_id=1, replica_groups=mesh['grp'=8,'sub'=16] {'grp','sub'}, use_global_device_ids=true, to_apply=%region_16.17 | all-reduce | flops 64 | bytes 512 | tf_op jit(solution)/shard_map/psum | solution.py:94
  (166 shorter events, 216.8 us)
Async XLA Ops:
  5.7 13.8 %all-to-all-start = ((s32[8,1,1296]{2,1,0:T(1,128)}), s32[8,1,1296]{2,1,0:T(1,128)S(1)}, u32[]{:S(2)}, u32[]{:S(2)}) async-start(s32[8,1,1296]{2,1,0:T(1,128)} %reshape.81), calls=%async_computation | async-start | bytes 90112 | tf_op jit(solution)/shard_map/all_to_all | solution.py:74
  19.5 4.9 copy-start
  19.5 63.7 %all-to-all-start.1 = ((bf16[8,48,6656]{2,1,0:T(8,128)(2,1)}), bf16[8,48,6656]{2,1,0:T(8,128)(2,1)}, u32[]{:S(2)}, u32[]{:S(2)}) async-start(bf16[8,48,6656]{2,1,0:T(8,128)(2,1)} %bitcast.68), calls=%async_computation.1 | async-start | bytes 10223616 | tf_op jit(solution)/shard_map/all_to_all | solution.py:73
  24.4 5.4 %collective-permute-start = (bf16[96,256]{1,0:T(8,128)(2,1)S(1)}, bf16[96,256]{1,0:T(8,128)(2,1)S(1)}, u32[]{:S(2)}, u32[]{:S(2)}) collective-permute-start(bf16[96,256]{1,0:T(8,128)(2,1)S(1)} %slice.28), channel_id=1, source_target_pairs={{1,0},{2,1},{3,2},{4,3},{5,4},{6,5},{7,6},{8,7},{9,8},{10,9},{11,1... | collective-permute-start | bytes 147464 | tf_op jit(solution)/shard_map/ppermute | solution.py:13
  246.8 4.8 collective-permute-start.1
  321.9 4.8 collective-permute-start.2
  439.9 4.1 collective-permute-start.3
where the time goes:
time: 520 us; the launch traced here: 516 us
  matrix products  147 us (28%)
  local copies, waits for them, and re-layouts  141 us (27%)
  blocking collectives  135 us (26%)
  waiting for transfers between devices  61.3 us (12%)
  starting transfers between devices  20.5 us (4%)
  other arithmetic  9.82 us (2%)
    psum x2, blocking collectives, shards(): lax.psum((column_sums(residual, image), column_sums(image, image)), ('grp...  135 us
    all_to_all x1, waiting for transfers between devices, shards(): lax.all_to_all(send_blocks, 'grp', split_axis=0, concat_axis=0, tiled=True)  53.3 us
    unnamed x7, local copies, waits for them, and re-layouts  52.2 us
    dot_general x16, matrix products, one_group(): jnp.einsum('spcqd,cosp->dosq', matrix, picked, preferred_element_type=jnp...  44.9 us
    dot_general x16, matrix products, one_group(): acc = acc + jnp.dot(high_part, selector, preferred_element_type=jnp.float32)  39.2 us
    dot_general x16, matrix products, one_group(): acc = acc + jnp.dot(low_part, selector, preferred_element_type=jnp.float32)  37.2 us
    reshape x16, local copies, waits for them, and re-layouts, one_group(): picked = picked.reshape(3, rows // 3, slot_count, 27)  26.4 us
    dot_general x16, matrix products, one_group(): jnp.einsum('rw,lw->rl', field, selector, preferred_element_type=jnp.float32)  25.1 us
  transfers between devices with their start and end apart: 6, of which 5 were waited for; matrix products, arithmetic and copies ran while one was open for 2% of the time, Pallas kernels for 0%

commit v1 on v0

--- a/solution.py
+++ b/solution.py
@@ -92,7 +92,7 @@
             incoming, ((0, 0), (0, own_count - band_width))
         )
         along, energy = lax.psum(
-            (column_sums(residual, image), column_sums(image, image)), ("grp", "sub")
+            lax.psum((column_sums(residual, image), column_sums(image, image)), "sub"), "grp"
         )
         solution, residual = update(solution, residual, image, along, energy)
     return (solution, residual)

time: 520 us -> 491 us (0.944)
  blocking collectives: 135 us -> 107 us
    psum x2 -> x4, blocking collectives: 135 us -> 107 us  [the longest x2 65 us: shards(): lax.psum((column_sums(residual, image), column_sums(image, image)), 'sub')]
where the time goes in v1:
time: 491 us; the launch traced here: 487 us
  matrix products  147 us (30%)
  local copies, waits for them, and re-layouts  141 us (29%)
  blocking collectives  107 us (22%)
  waiting for transfers between devices  61.3 us (12%)
  starting transfers between devices  19.5 us (4%)
  other arithmetic  9.83 us (2%)
    psum x2, blocking collectives, shards(): lax.psum((column_sums(residual, image), column_sums(image, image)), 'sub')  65 us
    all_to_all x1, waiting for transfers between devices, shards(): lax.all_to_all(send_blocks, 'grp', split_axis=0, concat_axis=0, tiled=True)  53.3 us
    unnamed x7, local copies, waits for them, and re-layouts  52.2 us
    dot_general x16, matrix products, one_group(): jnp.einsum('spcqd,cosp->dosq', matrix, picked, preferred_element_type=jnp...  44.9 us
    psum x2, blocking collectives, shards(): lax.psum(lax.psum((column_sums(residual, image), column_sums(image, image...  42 us
    dot_general x16, matrix products, one_group(): acc = acc + jnp.dot(high_part, selector, preferred_element_type=jnp.float32)  39.2 us
    dot_general x16, matrix products, one_group(): acc = acc + jnp.dot(low_part, selector, preferred_element_type=jnp.float32)  37.2 us
    reshape x16, local copies, waits for them, and re-layouts, one_group(): picked = picked.reshape(3, rows // 3, slot_count, 27)  26.4 us
  transfers between devices with their start and end apart: 6, of which 5 were waited for; matrix products, arithmetic and copies ran while one was open for 2% of the time, Pallas kernels for 0%

profile of v1, /device:TPU:1, one launch (start us, length us, event | category | flops | bytes accessed | tf_op | source)
XLA Modules:
  0.0 486.9 jit_solution(6607161550965911844)
XLA Ops:
  5.7 6.8 %all-to-all-start = ((s32[8,1,1296]{2,1,0:T(1,128)}), s32[8,1,1296]{2,1,0:T(1,128)S(1)}, u32[]{:S(2)}, u32[]{:S(2)}) async-start(s32[8,1,1296]{2,1,0:T(1,128)} %reshape.81), calls=%async_computation | async-start | bytes 90112 | tf_op jit(solution)/shard_map/all_to_all | solution.py:74
  12.5 6.9 %scatter_custom_fusion.1 = bf16[384,6656]{1,0:T(8,128)(2,1)} fusion(s32[128]{0:T(128)S(1)} %fusion.50, bf16[128,6656]{1,0:T(8,128)(2,1)} %param.9, bf16[]{:T(256)} %constant.23.clone.1), kind=kCustom, calls=%fused_computation.46 | custom fusion | bytes 5112320 | tf_op jit(solution)/shard_map/scatter | solution.py:25
  19.5 4.9 %all-to-all-start.1 = ((bf16[8,48,6656]{2,1,0:T(8,128)(2,1)}), bf16[8,48,6656]{2,1,0:T(8,128)(2,1)}, u32[]{:S(2)}, u32[]{:S(2)}) async-start(bf16[8,48,6656]{2,1,0:T(8,128)(2,1)} %bitcast.68), calls=%async_computation.1 | async-start | bytes 10223616 | tf_op jit(solution)/shard_map/all_to_all | solution.py:73
  29.8 53.3 %all-to-all-done.1 = bf16[8,48,6656]{2,1,0:T(8,128)(2,1)} async-done(((bf16[8,48,6656]{2,1,0:T(8,128)(2,1)}), bf16[8,48,6656]{2,1,0:T(8,128)(2,1)}, u32[]{:S(2)}, u32[]{:S(2)}) %all-to-all-start.1) | async-done | bytes 5111840 | tf_op jit(solution)/shard_map/all_to_all | solution.py:73
  83.1 14.8 %copy.45 = bf16[8,48,6561]{1,0,2:T(8,128)(2,1)} copy(bf16[8,48,6561]{2,1,0:T(8,128)(2,1)} %bitcast.44) | data formatting | bytes 10077696
  97.9 35.7 %copy.35 = bf16[8,48,27,3,27,3]{4,2,3,5,1,0:T(8,128)(2,1)} copy(bf16[8,48,27,3,27,3]{1,0,5,4,3,2:T(8,128)(2,1)} %bitcast.67) | data formatting | bytes 10077696
  133.6 112.3 %while.22 = (s32[]{:T(128)}, f32[96,1280]{1,0:T(8,128)}, s32[8,1296]{1,0:T(8,128)}, bf16[96,1280]{1,0:T(8,128)(2,1)S(1)}, bf16[8,48,27,3,27,3]{4,2,3,5,1,0:T(8,128)(2,1)}, /*index=5*/s32[]{:T(128)}, s32[]{:T(128)}) while((s32[]{:T(128)}, f32[96,1280]{1,0:T(8,128)}, s32[8,1296]{1,0:T(8,128)}, bf16[96,1280]{1,0:T(8,128)(2,1)S(1)}, ...), condition=%wide.region_5.6_spmd.clone, body=%wide.region_4.5_spmd.clone.sunk | while | flops 981762048 | bytes 10256283 | solution.py:53
  137.7 2.8 fusion.75
  150.8 2.8 fusion.75
  165.0 2.8 fusion.75
  179.1 2.8 fusion.75
  193.3 2.8 fusion.75
  207.5 2.8 fusion.75
  221.6 2.8 fusion.75
  235.8 2.8 fusion.75
  246.8 3.2 collective-permute-start.1
  253.0 34.3 %all-reduce.3 = (f32[32]{0:T(128)S(1)}, f32[32]{0:T(128)S(1)}) all-reduce(f32[32]{0:T(128)S(1)} %reduce_sum.62, f32[32]{0:T(128)S(1)} %reduce_sum.82), channel_id=1, replica_groups=mesh['grp'=8,'sub'=16] {'sub'}, use_global_device_ids=true, to_apply=%region_8.9 | all-reduce | flops 64 | bytes 512 | tf_op jit(solution)/shard_map/psum | solution.py:95
  287.3 20.7 %all-reduce.5 = (f32[32]{0:T(128)S(1)}, f32[32]{0:T(128)S(1)}) all-reduce(f32[32]{0:T(128)S(1)} %get-tuple-element.164, f32[32]{0:T(128)S(1)} %get-tuple-element.165), channel_id=1, replica_groups=mesh['grp'=8,'sub'=16] {'grp'}, use_global_device_ids=true, to_apply=%region_9.10 | all-reduce | flops 64 | bytes 512 | tf_op jit(solution)/shard_map/psum | solution.py:94
  311.5 3.3 collective-permute-done.2
  314.8 112.3 %while.23 = (s32[]{:T(128)}, f32[96,1280]{1,0:T(8,128)}, s32[8,1296]{1,0:T(8,128)}, bf16[96,1280]{1,0:T(8,128)(2,1)S(1)}, bf16[8,48,27,3,27,3]{4,2,3,5,1,0:T(8,128)(2,1)}, /*index=5*/s32[]{:T(128)}, s32[]{:T(128)}) while((s32[]{:T(128)}, f32[96,1280]{1,0:T(8,128)}, s32[8,1296]{1,0:T(8,128)}, bf16[96,1280]{1,0:T(8,128)(2,1)S(1)}, ...), condition=%wide.region_15.16_spmd.clone, body=%wide.region_14.15_spmd.clone.sunk | while | flops 981762048 | bytes 10256283 | solution.py:53
  318.9 2.8 fusion.83
  332.0 2.8 fusion.83
  432.7 30.6 %all-reduce.2 = (f32[32]{0:T(128)S(1)}, f32[32]{0:T(128)S(1)}) all-reduce(f32[32]{0:T(128)S(1)} %reduce_sum.85, f32[32]{0:T(128)S(1)} %reduce_sum.88), channel_id=1, replica_groups=mesh['grp'=8,'sub'=16] {'sub'}, use_global_device_ids=true, to_apply=%region_18.19 | all-reduce | flops 64 | bytes 512 | tf_op jit(solution)/shard_map/psum | solution.py:95
  463.4 21.3 %all-reduce.4 = (f32[32]{0:T(128)S(1)}, f32[32]{0:T(128)S(1)}) all-reduce(f32[32]{0:T(128)S(1)} %get-tuple-element.162, f32[32]{0:T(128)S(1)} %get-tuple-element.163), channel_id=1, replica_groups=mesh['grp'=8,'sub'=16] {'grp'}, use_global_device_ids=true, to_apply=%region_19.20 | all-reduce | flops 64 | bytes 512 | tf_op jit(solution)/shard_map/psum | solution.py:94
  (168 shorter events, 221.5 us)
Async XLA Ops:
  5.7 13.8 %all-to-all-start = ((s32[8,1,1296]{2,1,0:T(1,128)}), s32[8,1,1296]{2,1,0:T(1,128)S(1)}, u32[]{:S(2)}, u32[]{:S(2)}) async-start(s32[8,1,1296]{2,1,0:T(1,128)} %reshape.81), calls=%async_computation | async-start | bytes 90112 | tf_op jit(solution)/shard_map/all_to_all | solution.py:74
  19.5 4.9 %copy-start = (f32[96,1024]{1,0:T(8,128)S(1)}, f32[96,1024]{1,0:T(8,128)}, u32[]{:S(2)}) copy-start(f32[96,1024]{1,0:T(8,128)} %param.8) | copy-start | bytes 1179652
  19.5 63.7 %all-to-all-start.1 = ((bf16[8,48,6656]{2,1,0:T(8,128)(2,1)}), bf16[8,48,6656]{2,1,0:T(8,128)(2,1)}, u32[]{:S(2)}, u32[]{:S(2)}) async-start(bf16[8,48,6656]{2,1,0:T(8,128)(2,1)} %bitcast.68), calls=%async_computation.1 | async-start | bytes 10223616 | tf_op jit(solution)/shard_map/all_to_all | solution.py:73
  24.4 5.4 %collective-permute-start = (bf16[96,256]{1,0:T(8,128)(2,1)S(1)}, bf16[96,256]{1,0:T(8,128)(2,1)S(1)}, u32[]{:S(2)}, u32[]{:S(2)}) collective-permute-start(bf16[96,256]{1,0:T(8,128)(2,1)S(1)} %slice.28), channel_id=1, source_target_pairs={{1,0},{2,1},{3,2},{4,3},{5,4},{6,5},{7,6},{8,7},{9,8},{10,9},{11,1... | collective-permute-start | bytes 147464 | tf_op jit(solution)/shard_map/ppermute | solution.py:13
  246.8 4.8 collective-permute-start.1
  310.0 4.8 collective-permute-start.2
  428.0 3.2 collective-permute-start.3
